TPU v7x, 32 devices: a whole 2x2x4 slice. The times are simulated.
32 devices in a mesh: krow: 16 (over z, y, x), col: 2 (over core).
Axes of the slice: x: 2, y: 2, z: 4, core: 2. Of those that a mesh axis runs over, the one named last changes fastest.
Arguments:
- features: bfloat16 [8192, 6144], P('krow', 'col'), may hold values from -9 to 9
- slab: bfloat16 [8192, 512], P('krow', 'col'), may hold values from -9 to 9
- pack_order: int32 [16, 512], P('krow'), may hold values from 0 to 511, each once within a row
- place_order: int32 [16, 512], P('krow'), may hold values from 0 to 511, each once within a row
- start: int32 [1], replicated, may hold values from 128 to 512
Outputs:
- factored: float32 [8192, 1024], P(('krow', 'col'))
Inputs may be any that keep to these rules, and one draw needn't show every extreme that they name: Row k of krow device s's sending order is its local row pack_order[s, k]. `place_order`: each krow device's elimination rows are a rearrangement of the rows it receives. Slab columns from start[0] on are not yet computed and are ignored.
All inputs are finite; a program needn't handle non-finite values.
Results may differ from a plain program's by a relative error of at most 0.0003.
Values may be sent and summed in bfloat16 or wider, within the bound.
A program may use at most 64 MiB of HBM per device.

v0:
```python
import jax
import jax.numpy as jnp
from jax import lax
from jax.sharding import PartitionSpec as P

F = 6144
PW = 512


RIDGE = 0.5


def spread(value, axis, source):
    kept = jnp.where(lax.axis_index(axis) == source, value, 0).astype(value.dtype)
    return lax.psum(kept, axis)


def shards(features, slab, pack_order, place_order, start):
    rows_dev = features.shape[0]
    prior_dev = slab.shape[1]
    column_ranks = lax.axis_size("col")
    krow_index = lax.axis_index("krow")
    col_index = lax.axis_index("col")
    packed = jnp.take(features, pack_order[0], axis=0)
    arrived = lax.all_to_all(packed, "krow", split_axis=0, concat_axis=0, tiled=True)
    ordered = jnp.take(arrived, place_order[0], axis=0)
    own_norms = jnp.sum(jnp.square(ordered.astype(jnp.float32)), axis=1)
    positions = krow_index * rows_dev + jnp.arange(rows_dev)
    kept = (col_index * prior_dev + jnp.arange(prior_dev) < start[0])[None, :]
    identity = jnp.eye(PW, dtype=jnp.float32)
    highest = lax.Precision.HIGHEST
    earlier = None
    pieces = []
    for panel in range(2):
        lower = panel * PW
        root = lower // rows_dev
        is_root = krow_index == root
        panel_feats, panel_slab = (spread(ordered, "krow", root), spread(slab, "krow", root))
        panel_slab = jnp.where(kept, panel_slab, jnp.zeros((), jnp.bfloat16))
        panel_norms = jnp.sum(jnp.square(panel_feats.astype(jnp.float32)), axis=1)
        gram = jnp.dot(ordered, panel_feats.T, preferred_element_type=jnp.float32)
        dist_part = own_norms[:, None] + panel_norms[None, :] - 2.0 * gram
        update_part = jnp.dot(slab, panel_slab.T, preferred_element_type=jnp.float32)
        dist, update = lax.psum((dist_part, update_part), "col")
        targets = lower + jnp.arange(PW)
        shift = (positions[:, None] == targets[None, :]).astype(jnp.float32)
        matrix = jnp.exp(-dist / (2.0 * F)) + RIDGE * shift - update
        if panel == 0:
            block = matrix
            factor = spread(jnp.linalg.cholesky(jnp.where(is_root, block, identity)), "krow", root)
        else:
            block = matrix
            block = block - jnp.dot(earlier, earlier.T, precision=highest)
            local_factor = jnp.linalg.cholesky(jnp.where(is_root, block, identity))
            factor, remote = (spread(local_factor, "krow", root), spread(earlier, "krow", root))
            matrix = matrix - jnp.dot(earlier, remote.T, precision=highest)
        solved = jax.scipy.linalg.solve_triangular(factor, matrix.T, lower=True).T
        solved = jnp.where((positions >= lower)[:, None], solved, jnp.zeros((), jnp.float32))
        earlier = solved
        pieces.append(solved)
    whole = jnp.concatenate(pieces, axis=1)
    part_rows = rows_dev // column_ranks
    return lax.dynamic_slice_in_dim(whole, col_index * part_rows, part_rows, 0)


def solution(mesh):
    in_specs = (P("krow", "col"), P("krow", "col"), P("krow", None), P("krow", None), P())
    out_specs = P(("krow", "col"), None)
    return jax.shard_map(shards, mesh=mesh, in_specs=in_specs, out_specs=out_specs, check_vma=False)
```

profile of v0, /device:TPU:0, one launch (start us, length us, event | category | flops | bytes accessed | tf_op | source)
XLA Modules:
  0.0 918.2 jit_solution(11058304098605848518)
XLA Ops:
  8.4 3.8 gather_fusion
  12.3 3.9 broadcast_select_fusion.1
  16.2 8.5 all-to-all-start
  25.6 59.9 %all-to-all-done = bf16[16,32,3072]{2,1,0:T(8,128)(2,1)S(1)} async-done(((bf16[16,32,3072]{2,1,0:T(8,128)(2,1)}), bf16[16,32,3072]{2,1,0:T(8,128)(2,1)S(1)}, u32[]{:S(2)}, u32[]{:S(2)}) %all-to-all-start) | async-done | bytes 3145760 | tf_op jit(solution)/shard_map/all_to_all | solution.py:25
  85.5 3.8 gather_fusion.1
  89.3 5.1 broadcast_select_fusion.2
  97.3 228.4 %all-reduce.15.cloned.1.call-done = (bf16[512,256]{1,0:T(8,128)(2,1)}, bf16[512,3072]{1,0:T(8,128)(2,1)}, bf16[512,256]{1,0:T(8,128)(2,1)}, bf16[512,3072]{1,0:T(8,128)(2,1)}) async-done(((bf16[512,256]{1,0:T(8,128)(2,1)}, bf16[512,3072]{1,0:T(8,128)(2,1)}, bf16[512,256]{1,0:T(8,128)(2,1)}, bf16[512,3072]{1,0:T(8,128)(2,1)}), (bf16[512,256]{1,0:T(8,128)(2,1)}, bf16[512,3072]{1,0:T(8,128)(2,1)}, ...) | async-done | bytes 6815760 | tf_op jit(solution)/shard_map/psum | solution.py:15
  329.4 3.0 fusion.2
  332.4 3.0 fusion.1
  338.3 27.5 %all-reduce.13.cloned.1.call-done = (f32[512,512]{0,1:T(8,128)}, f32[512,512]{0,1:T(8,128)}, f32[512,512]{0,1:T(8,128)}, f32[512,512]{0,1:T(8,128)}) async-done(((f32[512,512]{0,1:T(8,128)}, f32[512,512]{0,1:T(8,128)}, f32[512,512]{0,1:T(8,128)}, f32[512,512]{0,1:T(8,128)}), (f32[512,512]{0,1:T(8,128)}, f32[512,512]{0,1:T(8,128)}, f32[512,512]{0,1:T(8,128)}, ...) | async-done | bytes 4194320 | tf_op jit(solution)/shard_map/psum | solution.py:44
  369.3 11.7 %cholesky.286 = f32[128,128]{1,0:T(8,128)S(1)} custom-call(f32[128,128]{1,0:T(8,128)S(1)} %cholesky.426), custom_call_target="Cholesky" | custom-call | tf_op jit(solution)/shard_map/jit(cholesky)/cholesky | solution.py:50
  381.0 9.8 %custom-call.27 = f32[1,128,128]{1,2,0:T(8,128)S(1)} custom-call(f32[1,128,128]{2,1,0:T(8,128)S(1)} %get-tuple-element.79), custom_call_target="InvertDiagBlocksLowerTriangular" | custom-call | tf_op jit(solution)/shard_map/jit(cholesky)/cholesky | solution.py:50
  393.4 11.7 %cholesky.305 = f32[128,128]{1,0:T(8,128)S(1)} custom-call(f32[128,128]{1,0:T(8,128)S(1)} %cholesky.430), custom_call_target="Cholesky" | custom-call | tf_op jit(solution)/shard_map/jit(cholesky)/cholesky | solution.py:50
  405.5 10.2 %custom-call.28 = f32[1,128,128]{1,2,0:T(8,128)S(1)} custom-call(f32[1,128,128]{2,1,0:T(8,128)S(1)} %get-tuple-element.77), custom_call_target="InvertDiagBlocksLowerTriangular" | custom-call | tf_op jit(solution)/shard_map/jit(cholesky)/cholesky | solution.py:50
  417.7 11.7 %cholesky.326 = f32[128,128]{1,0:T(8,128)S(1)} custom-call(f32[128,128]{1,0:T(8,128)S(1)} %cholesky.435), custom_call_target="Cholesky" | custom-call | tf_op jit(solution)/shard_map/jit(cholesky)/cholesky | solution.py:50
  429.5 9.8 %custom-call.29 = f32[1,128,128]{1,2,0:T(8,128)S(1)} custom-call(f32[1,128,128]{2,1,0:T(8,128)S(1)} %get-tuple-element.75), custom_call_target="InvertDiagBlocksLowerTriangular" | custom-call | tf_op jit(solution)/shard_map/jit(cholesky)/cholesky | solution.py:50
  441.0 11.9 %cholesky.343 = f32[128,128]{1,0:T(8,128)S(1)} custom-call(f32[128,128]{1,0:T(8,128)S(1)} %convolution_subtract_fusion.13), custom_call_target="Cholesky" | custom-call | tf_op jit(solution)/shard_map/jit(cholesky)/cholesky | solution.py:50
  459.3 113.7 %all-reduce.9.cloned.1.call-done = f32[512,512]{0,1:T(8,128)} async-done(((f32[512,512]{0,1:T(8,128)}), f32[512,512]{0,1:T(8,128)}) %all-reduce.9.cloned.1.call-update) | async-done | bytes 1048592 | tf_op jit(solution)/shard_map/psum | solution.py:15
  574.4 8.4 while.4
  582.7 39.3 %custom-call.30 = f32[4,128,128]{1,2,0:T(8,128)S(1)} custom-call(f32[4,128,128]{2,1,0:T(8,128)S(1)} %get-tuple-element.22), custom_call_target="InvertDiagBlocksLowerTriangular" | custom-call | tf_op jit(solution)/shard_map/jit(_solve_triangular)/triangular_solve | solution.py:57
  626.8 3.8 convert_select_fusion
  632.1 11.7 %cholesky.358 = f32[128,128]{1,0:T(8,128)S(1)} custom-call(f32[128,128]{1,0:T(8,128)S(1)} %cholesky.439), custom_call_target="Cholesky" | custom-call | tf_op jit(solution)/shard_map/jit(cholesky)/cholesky | solution.py:54
  644.0 9.8 %custom-call.31 = f32[1,128,128]{1,2,0:T(8,128)S(1)} custom-call(f32[1,128,128]{2,1,0:T(8,128)S(1)} %get-tuple-element.73), custom_call_target="InvertDiagBlocksLowerTriangular" | custom-call | tf_op jit(solution)/shard_map/jit(cholesky)/cholesky | solution.py:54
  656.5 11.7 %cholesky.377 = f32[128,128]{1,0:T(8,128)S(1)} custom-call(f32[128,128]{1,0:T(8,128)S(1)} %cholesky.443), custom_call_target="Cholesky" | custom-call | tf_op jit(solution)/shard_map/jit(cholesky)/cholesky | solution.py:54
  669.6 9.8 %custom-call.32 = f32[1,128,128]{1,2,0:T(8,128)S(1)} custom-call(f32[1,128,128]{2,1,0:T(8,128)S(1)} %get-tuple-element.70), custom_call_target="InvertDiagBlocksLowerTriangular" | custom-call | tf_op jit(solution)/shard_map/jit(cholesky)/cholesky | solution.py:54
  681.0 11.7 %cholesky.398 = f32[128,128]{1,0:T(8,128)S(1)} custom-call(f32[128,128]{1,0:T(8,128)S(1)} %cholesky.448), custom_call_target="Cholesky" | custom-call | tf_op jit(solution)/shard_map/jit(cholesky)/cholesky | solution.py:54
  693.4 10.2 %custom-call.33 = f32[1,128,128]{1,2,0:T(8,128)S(1)} custom-call(f32[1,128,128]{2,1,0:T(8,128)S(1)} %get-tuple-element.67), custom_call_target="InvertDiagBlocksLowerTriangular" | custom-call | tf_op jit(solution)/shard_map/jit(cholesky)/cholesky | solution.py:54
  705.0 11.7 %cholesky.415 = f32[128,128]{1,0:T(8,128)S(1)} custom-call(f32[128,128]{1,0:T(8,128)S(1)} %convolution_subtract_fusion.12), custom_call_target="Cholesky" | custom-call | tf_op jit(solution)/shard_map/jit(cholesky)/cholesky | solution.py:54
  722.6 124.8 %all-reduce.11.cloned.1.call-done = (f32[512,512]{1,0:T(8,128)}, f32[512,512]{1,0:T(8,128)}) async-done(((f32[512,512]{1,0:T(8,128)}, f32[512,512]{1,0:T(8,128)}), (f32[512,512]{1,0:T(8,128)}, f32[512,512]{1,0:T(8,128)})) %all-reduce.11.cloned.1.call-update) | async-done | bytes 2097168 | tf_op jit(solution)/shard_map/psum | solution.py:15
  848.7 7.5 while.5
  856.2 40.1 %custom-call.34 = f32[4,128,128]{1,2,0:T(8,128)} custom-call(f32[4,128,128]{2,1,0:T(8,128)S(1)} %get-tuple-element.23), custom_call_target="InvertDiagBlocksLowerTriangular" | custom-call | tf_op jit(solution)/shard_map/jit(_solve_triangular)/triangular_solve | solution.py:57
  896.3 4.0 fusion
  (168 shorter events, 72.2 us)
Async XLA Ops:
  6.5 1.9 copy-start
  16.2 8.5 copy-start.14
  16.2 8.6 copy-start.9
  16.2 69.3 %all-to-all-start = ((bf16[16,32,3072]{2,1,0:T(8,128)(2,1)}), bf16[16,32,3072]{2,1,0:T(8,128)(2,1)S(1)}, u32[]{:S(2)}, u32[]{:S(2)}) async-start(bf16[16,32,3072]{2,1,0:T(8,128)(2,1)} %bitcast.119), calls=%async_computation | async-start | bytes 6291456 | tf_op jit(solution)/shard_map/all_to_all | solution.py:25
  24.6 301.0 %all-reduce.15.cloned.1.call-start = ((), (), s32[]{:S(2)}) async-start(), calls=%async_computation.4 | async-start | bytes 13631488 | tf_op jit(solution)/shard_map/psum | solution.py:15
  94.4 1.9 copy-start.2
  94.4 271.4 %all-reduce.13.cloned.1.call-start = ((), (), s32[]{:S(2)}) async-start(), calls=%async_computation.3 | async-start | bytes 8388608 | tf_op jit(solution)/shard_map/psum | solution.py:44
  325.6 2.8 copy-start.5
  325.6 3.8 copy-start.6
  332.4 3.0 copy-start.13
  332.4 4.3 copy-start.12
  338.1 234.9 %all-reduce.9.cloned.1.call-start = ((), (), s32[]{:S(2)}) async-start(), calls=%async_computation.1 | async-start | bytes 2097152 | tf_op jit(solution)/shard_map/psum | solution.py:15
  368.3 1.0 copy-start.8
  459.2 388.2 %all-reduce.11.cloned.1.call-start = ((), (), s32[]{:S(2)}) async-start(), calls=%async_computation.2 | async-start | bytes 4194304 | tf_op jit(solution)/shard_map/psum | solution.py:15
  622.0 1.8 copy-start.11
  631.1 1.0 copy-start.7
  896.3 4.0 copy-start.10
  901.6 0.9 copy-start.4
  904.7 6.8 copy-start.1
  907.5 2.9 copy-start.3
Sparse Core Ops, SparseCore 0:
  94.6 231.0 all-reduce.14
  338.2 27.5 all-reduce.12
  459.3 113.6 all-reduce.8
  721.6 125.7 all-reduce.10
where the time goes:
time: 926 us; the launch traced here: 918 us
  waiting for transfers between devices  554 us (60%)
  other arithmetic  265 us (29%)
  matrix products  37.3 us (4%)
  local copies, waits for them, and re-layouts  32.4 us (3%)
  between operations  19.8 us (2%)
    psum x3, waiting for transfers between devices, spread(): return lax.psum(kept, axis)  467 us
    another operation x5, other arithmetic, shards(): solved = jax.scipy.linalg.solve_triangular(factor, matrix.T, lower=True).T  82.1 us
    another operation x15, other arithmetic, shards(): jnp.linalg.cholesky(jnp.where(is_root, block, identity))  79.5 us
    another operation x15, other arithmetic, shards(): local_factor = jnp.linalg.cholesky(jnp.where(is_root, block, identity))  79.4 us
    all_to_all x1, waiting for transfers between devices, shards(): lax.all_to_all(packed, 'krow', split_axis=0, concat_axis=0, tiled=True)  59.9 us
    psum x1, waiting for transfers between devices, shards(): dist, update = lax.psum((dist_part, update_part), 'col')  27.5 us
    another operation x41, local copies, waits for them, and re-layouts, shards(): solved = jax.scipy.linalg.solve_triangular(factor, matrix.T, lower=True).T  19.7 us
  transfers between devices with their start and end apart: 5, of which 5 were waited for; matrix products, arithmetic and copies ran while one was open for 0% of the time, Pallas kernels for 0%

commit v1 on v0

v1 whole, which is shorter than its diff:
```python
import jax
import jax.numpy as jnp
from jax import lax
from jax.experimental import pallas as pl
from jax.experimental.pallas import tpu as pltpu
from jax.sharding import PartitionSpec as P

F = 6144
PW = 512
RIDGE = 0.5
T = 128
HI = lax.Precision.HIGHEST
NT = (((1,), (1,)), ((), ()))


def dot_nt(a, b):
    return lax.dot_general(a, b, NT, precision=HI, preferred_element_type=jnp.float32)


def inverse_factor(block):
    shape = (T, T)
    rows = lax.broadcasted_iota(jnp.int32, shape, 0)
    lanes = lax.broadcasted_iota(jnp.int32, shape, 1)
    a = block
    z = (rows == lanes).astype(jnp.float32)
    done = []
    for low in range(0, T, 8):
        n = T - low
        sub = lax.broadcasted_iota(jnp.int32, (n, T), 0)
        cols = [jnp.broadcast_to(a[:, low + m:low + m + 1], (n, T)) for m in range(8)]
        pivots = jnp.ones((8, T), jnp.float32)
        for j in range(8):
            pivot = cols[j][j:j + 1, :]
            scale = jnp.where(sub > j, cols[j] * (1.0 / pivot), 0.0)
            for m in range(j + 1, 8):
                cols[m] = cols[m] - scale * cols[m][j:j + 1, :]
            if n > 8:
                a = a - scale * a[j:j + 1, :]
            z = z - scale * z[j:j + 1, :]
            pivots = jnp.where(sub[:8] == j, pivot, pivots)
        done.append(z[:8] * lax.rsqrt(pivots))
        a, z = a[8:], z[8:]
    return jnp.concatenate(done, axis=0)


def factor_kernel(top_ref, low_ref, inv_ref):
    size = top_ref.shape[0]
    blocks = size // T
    low_ref[...] = top_ref[...]
    ids = lax.broadcasted_iota(jnp.int32, (size, T), 0)

    def step(k, carry):
        at = pl.ds(pl.multiple_of(k * T, T), T)
        inv = inverse_factor(low_ref[at, at])
        inv_ref[at, :] = inv
        col = dot_nt(low_ref[:, at], inv)
        col = jnp.where(ids >= (k + 1) * T, col, 0.0)
        low_ref[:, at] = col

        def trail(i, c):
            rows = pl.ds(pl.multiple_of(i * T, T), T)
            low_ref[rows, :] = low_ref[rows, :] - dot_nt(low_ref[rows, at], low_ref[:, at])
            return c

        return lax.fori_loop(k + 1, blocks, trail, carry)

    lax.fori_loop(0, blocks, step, 0)


def factor(top):
    size = top.shape[0]
    return pl.pallas_call(
        factor_kernel,
        out_shape=(
            jax.ShapeDtypeStruct((size, size), jnp.float32),
            jax.ShapeDtypeStruct((size, T), jnp.float32),
        ),
        in_specs=[pl.BlockSpec(memory_space=pltpu.VMEM)],
        out_specs=(pl.BlockSpec(memory_space=pltpu.VMEM),) * 2,
        compiler_params=pltpu.CompilerParams(vmem_limit_bytes=40 * 2**20),
        cost_estimate=pl.CostEstimate(flops=2 * 10**10, bytes_accessed=8 * size * size, transcendentals=0),
        name="factor",
    )(top)


def solve_kernel(mat_ref, low_ref, inv_ref, out_ref):
    size = low_ref.shape[0]
    out_ref[...] = mat_ref[...]

    def step(k, carry):
        at = pl.ds(pl.multiple_of(k * T, T), T)
        col = dot_nt(out_ref[:, at], inv_ref[at, :])
        out_ref[...] = out_ref[...] - dot_nt(col, low_ref[:, at])
        out_ref[:, at] = col
        return carry

    lax.fori_loop(0, size // T, step, 0)


def solve(mat, low, inv):
    return pl.pallas_call(
        solve_kernel,
        out_shape=jax.ShapeDtypeStruct(mat.shape, jnp.float32),
        in_specs=[pl.BlockSpec(memory_space=pltpu.VMEM)] * 3,
        out_specs=pl.BlockSpec(memory_space=pltpu.VMEM),
        compiler_params=pltpu.CompilerParams(vmem_limit_bytes=40 * 2**20),
        name="solve",
    )(mat, low, inv)


def rows_of(x, idx):
    return x.at[idx].get(mode="promise_in_bounds")


def shards(features, slab, pack_order, place_order, start):
    rows_dev, feats_dev = features.shape
    prior_dev = slab.shape[1]
    krows = lax.axis_size("krow")
    column_ranks = lax.axis_size("col")
    krow_index = lax.axis_index("krow")
    col_index = lax.axis_index("col")
    group = rows_dev // krows
    top_rows = 2 * PW
    roots = top_rows // rows_dev
    part_rows = rows_dev // column_ranks

    place = place_order[0]
    digits = jnp.stack([place % 128, place // 128], axis=1).astype(jnp.bfloat16)
    digits = jnp.pad(digits, ((0, 0), (0, 126)))
    owned = jnp.concatenate([slab, digits], axis=1)
    pieces = lax.all_to_all(owned, "krow", split_axis=0, concat_axis=0, tiled=True)
    packed = rows_of(features, pack_order[0])
    head = jnp.concatenate([packed[:roots * group], pieces[:roots * group]], axis=1)
    every = lax.all_gather(head, "krow", axis=0, tiled=False)

    extra = every[:, :, feats_dev:].reshape(krows, roots, group, -1)
    extra = jnp.transpose(extra, (1, 0, 2, 3)).reshape(top_rows, -1)
    top_slab = extra[:, :prior_dev]
    top_slab = lax.all_gather(top_slab, "col", axis=1, tiled=True)
    kept = (jnp.arange(top_slab.shape[1]) < start[0])[None, :]
    top_slab = jnp.where(kept, top_slab, jnp.zeros((), jnp.bfloat16))
    places = extra[:, prior_dev:prior_dev + 2].astype(jnp.int32)
    places = places[:, 0] + 128 * places[:, 1]
    owner = jnp.arange(top_rows) // rows_dev
    source = (places // group) * (roots * group) + owner * group + places % group
    top = rows_of(every.reshape(krows * roots * group, -1), source)[:, :feats_dev]
    top_norms = jnp.sum(jnp.square(top.astype(jnp.float32)), axis=1)

    def matrix_of(dist, prior, first):
        update = lax.dot_general(prior, top_slab, NT, preferred_element_type=jnp.float32)
        at = first + jnp.arange(dist.shape[0])
        shift = (at[:, None] == jnp.arange(top_rows)[None, :]).astype(jnp.float32)
        return jnp.exp(-dist / (2.0 * F)) + RIDGE * shift - update

    def dist_of(own, norms):
        gram = lax.dot_general(own, top, NT, preferred_element_type=jnp.float32)
        return norms[:, None] + top_norms[None, :] - 2.0 * gram

    top_dist = lax.psum(dist_of(top, top_norms), "col")
    low, inv = factor(matrix_of(top_dist, top_slab, 0))

    arrived = lax.all_to_all(packed, "krow", split_axis=0, concat_axis=0, tiled=True)
    ordered = rows_of(arrived, place)
    own_norms = jnp.sum(jnp.square(ordered.astype(jnp.float32)), axis=1)
    dist = lax.psum_scatter(dist_of(ordered, own_norms), "col", scatter_dimension=0, tiled=True)
    own_slab = lax.all_to_all(slab, "col", split_axis=0, concat_axis=1, tiled=True)
    first = krow_index * rows_dev + col_index * part_rows
    solved = solve(matrix_of(dist, own_slab, first), low, inv)
    at = first + jnp.arange(part_rows)
    lower = (jnp.arange(top_rows) // PW) * PW
    return jnp.where(at[:, None] >= lower[None, :], solved, 0.0)


def solution(mesh):
    in_specs = (P("krow", "col"), P("krow", "col"), P("krow", None), P("krow", None), P())
    out_specs = P(("krow", "col"), None)
    return jax.shard_map(shards, mesh=mesh, in_specs=in_specs, out_specs=out_specs, check_vma=False)
```

time: 926 us -> 323 us (0.35)
  waiting for transfers between devices: 554 us -> 146 us
  other arithmetic: 265 us -> 13.7 us
  Pallas kernels: 0 us -> 65 us
  matrix products: 37.3 us -> 27 us
    psum x4 -> x1, waiting for transfers between devices: 494 us -> 0.02 us  [shards(): top_dist = lax.psum(dist_of(top, top_norms), 'col')]
    another operation x35 -> x3, other arithmetic: 241 us -> 1.66 us  [the longest x5 82.1 us: shards(): solved = jax.scipy.linalg.solve_triangular(factor, matrix.T, lower=True).T]
    all_gather x0 -> x2, waiting for transfers between devices: none -> 139 us  [the longest x1 139 us: shards(): every = lax.all_gather(head, 'krow', axis=0, tiled=False)]
    pallas_call x0 -> x2, Pallas kernels: none -> 65 us  [the longest x1 54.2 us: factor(): pl.pallas_call(factor_kernel, out_shape=(jax.ShapeDtypeStruct((size, size...]
    all_to_all x1, waiting for transfers between devices: 59.9 us -> 0.01 us  [shards(): lax.all_to_all(packed, 'krow', split_axis=0, concat_axis=0, tiled=True)]
    gather x2 -> x3, local copies, waits for them, and re-layouts: 7.63 us -> 30.5 us  [rows_of(): return x.at[idx].get(mode='promise_in_bounds')]
    another operation x26 -> x0, matrix products: 20.9 us -> none  [the longest x14 9.28 us: shards(): solved = jax.scipy.linalg.solve_triangular(factor, matrix.T, lower=True).T]
    another operation x58 -> x0, local copies, waits for them, and re-layouts: 20.5 us -> none  [the longest x41 19.7 us: shards(): solved = jax.scipy.linalg.solve_triangular(factor, matrix.T, lower=True).T]
  transfers between devices with their start and end apart: 5 -> 7, of which waited for: 5 -> 3; matrix products, arithmetic and copies ran while one was open for 0% -> 21% of each run, Pallas kernels for 0% -> 17%
where the time goes in v1:
time: 323 us
  waiting for transfers between devices  146 us (45%)
  Pallas kernels  65 us (20%)
  local copies, waits for them, and re-layouts  39.8 us (12%)
  matrix products  27 us (8%)
  starting transfers between devices  16.9 us (5%)
  between operations  14 us (4%)
  other arithmetic  13.7 us (4%)
    all_gather x1, waiting for transfers between devices, shards(): every = lax.all_gather(head, 'krow', axis=0, tiled=False)  139 us
    pallas_call x1, Pallas kernels, factor(): pl.pallas_call(factor_kernel, out_shape=(jax.ShapeDtypeStruct((size, size...  54.2 us
    gather x3, local copies, waits for them, and re-layouts, rows_of(): return x.at[idx].get(mode='promise_in_bounds')  30.5 us
    dot_general x2, matrix products, dist_of(): gram = lax.dot_general(own, top, NT, preferred_element_type=jnp.float32)  20.5 us
    pallas_call x1, Pallas kernels, solve(): pl.pallas_call(solve_kernel, out_shape=jax.ShapeDtypeStruct(mat.shape, jn...  10.8 us
    all_to_all x1, starting transfers between devices, shards(): lax.all_to_all(owned, 'krow', split_axis=0, concat_axis=0, tiled=True)  8.39 us
    all_to_all x1, waiting for transfers between devices, shards(): lax.all_to_all(owned, 'krow', split_axis=0, concat_axis=0, tiled=True)  7.05 us
  transfers between devices with their start and end apart: 7, of which 3 were waited for; matrix products, arithmetic and copies ran while one was open for 21% of the time, Pallas kernels for 17%

profile of v1, /device:TPU:0, one launch (start us, length us, event | category | flops | bytes accessed | tf_op | source)
XLA Modules:
  0.0 322.8 jit_solution(3414352390010034547)
XLA Ops:
  6.5 0.8 fusion.30
  7.4 0.8 fusion.31
  8.4 1.7 fusion.25
  10.1 8.4 %all-to-all-start.1 = ((bf16[16,32,384]{2,1,0:T(8,128)(2,1)}), bf16[16,32,384]{2,1,0:T(8,128)(2,1)}, u32[]{:S(2)}, u32[]{:S(2)}) async-start(bf16[16,32,384]{2,1,0:T(8,128)(2,1)} %bitcast.6), calls=%async_computation.1 | async-start | bytes 786432 | tf_op jit(solution)/shard_map/all_to_all | solution.py:131
  18.6 0.7 compare_select_fusion.2
  19.3 3.9 %gather_fusion = bf16[512,3072]{1,0:T(8,128)(2,1)} fusion(bf16[512,3072]{1,0:T(8,128)(2,1)S(1)} %copy-done, s32[1024]{0:T(1024)S(1)} %pad_clamp_fusion.1), kind=kCustom, calls=%fused_computation | custom fusion | bytes 6293504 | tf_op jit(solution)/shard_map/gather | solution.py:112
  23.1 1.0 slice.42
  24.2 7.0 %all-to-all-done.1 = bf16[16,32,384]{2,1,0:T(8,128)(2,1)} async-done(((bf16[16,32,384]{2,1,0:T(8,128)(2,1)}), bf16[16,32,384]{2,1,0:T(8,128)(2,1)}, u32[]{:S(2)}, u32[]{:S(2)}) %all-to-all-start.1) | async-done | bytes 393248 | tf_op jit(solution)/shard_map/all_to_all | solution.py:131
  31.2 0.8 slice.43
  32.0 0.8 pad_maximum_fusion
  32.8 4.5 %all-to-all-start = ((bf16[16,32,3072]{2,1,0:T(8,128)(2,1)}), bf16[16,32,3072]{2,1,0:T(8,128)(2,1)}, u32[]{:S(2)}, u32[]{:S(2)}) async-start(bf16[16,32,3072]{2,1,0:T(8,128)(2,1)} %bitcast.40), calls=%async_computation | async-start | bytes 6291456 | tf_op jit(solution)/shard_map/all_to_all | solution.py:162
  37.4 138.6 %all-gather.6.cloned.1.call-done = bf16[1024,3456]{1,0:T(8,128)(2,1)} async-done(((bf16[64,3456]{1,0:T(8,128)(2,1)}), bf16[1024,3456]{1,0:T(8,128)(2,1)}) %all-gather.6.cloned.1.call-update) | async-done | bytes 7077904 | tf_op jit(solution)/shard_map/all_gather | solution.py:134
  176.0 1.2 slice.44
  177.3 0.9 fusion.21
  178.2 0.8 slice.49
  179.2 17.3 %gather_fusion.2 = bf16[1024,3456]{1,0:T(8,128)(2,1)} fusion(bf16[1024,3456]{1,0:T(8,128)(2,1)} %all-gather.6.cloned.1.call-done, s32[1024]{0:T(1024)S(1)} %broadcast_clamp_fusion), kind=kCustom, calls=%fused_computation.2 | custom fusion | bytes 14159872 | tf_op jit(solution)/shard_map/gather | solution.py:112
  196.5 4.1 %multiply_reduce_fusion = f32[1024]{0:T(1024)S(1)} fusion(bf16[1024,3456]{1,0:T(8,128)(2,1)} %gather_fusion.2), kind=kLoop, calls=%fused_computation.3 | loop fusion | flops 9436160 | bytes 6295552 | tf_op jit(solution)/shard_map/reduce_sum | solution.py:147
  200.5 12.0 %multiply_subtract_fusion = f32[1024,1024]{1,0:T(8,128)} fusion(bf16[1024,3456]{1,0:T(8,128)(2,1)} %gather_fusion.2, f32[1024]{0:T(1024)S(1)} %multiply_reduce_fusion), kind=kOutput, calls=%fused_computation.11 | convolution fusion | flops 6445596672 | bytes 10493952 | tf_op jit(solution)/shard_map/dot_general | solution.py:156
  212.9 9.4 %gather_fusion.1 = bf16[512,3072]{1,0:T(8,128)(2,1)} fusion(bf16[512,3072]{1,0:T(8,128)(2,1)} %bitcast.3, s32[1024]{0:T(1024)S(1)} %pad_clamp_fusion), kind=kCustom, calls=%fused_computation.1 | custom fusion | bytes 6293504 | tf_op jit(solution)/shard_map/gather | solution.py:112
  222.2 2.6 multiply_reduce_fusion.1
  224.8 8.5 %multiply_subtract_fusion.1 = f32[512,1024]{1,0:T(8,128)} fusion(bf16[512,3072]{1,0:T(8,128)(2,1)} %gather_fusion.1, bf16[1024,3456]{1,0:T(8,128)(2,1)} %gather_fusion.2, f32[1024]{0:T(1024)S(1)} %multiply_reduce_fusion, f32[512]{0:T(512)S(1)} %multiply_reduce_fusion.1), kind=kOutput, calls=%fused_computation.12 | convolution fusion | flops 3222798336 | bytes 11540480 | tf_op jit(solution)/shard_map/dot_general | solution.py:156
  233.3 3.7 %all-to-all-start.2 = ((bf16[2,256,256]{2,1,0:T(8,128)(2,1)}), bf16[2,256,256]{2,1,0:T(8,128)(2,1)S(1)}, u32[]{:S(2)}, u32[]{:S(2)}) async-start(bf16[2,256,256]{2,1,0:T(8,128)(2,1)} %bitcast.13), calls=%async_computation.3 | async-start | bytes 524288 | tf_op jit(solution)/shard_map/all_to_all | solution.py:166
  237.7 0.7 all-to-all-done.2
  238.4 0.8 copy.11
  239.3 4.2 %add_subtract_fusion.top_ref = f32[1024,1024]{1,0:T(8,128)S(1)} fusion(f32[1024,1024]{1,0:T(8,128)} %all-reduce.3.cloned.1.call-done, bf16[1024,512]{1,0:T(8,128)(2,1)} %all-gather.4.cloned.1.call-done, pred[512]{0:T(512)(128)(4,1)S(1)} %iota_compare_fusion.3), kind=kOutput, calls=%fused_computation.9 | convolution fusion | flops 1080557568 | bytes 9437696 | tf_op jit(solution)/shard_map/dot_general | solution.py:150
  243.5 54.2 %factor.1 = (f32[1024,1024]{1,0:T(8,128)S(1)}, f32[1024,128]{1,0:T(8,128)S(1)}) custom-call(f32[1024,1024]{1,0:T(8,128)S(1)} %add_subtract_fusion.top_ref), custom_call_target="tpu_custom_call" | custom-call | flops 20000000000 | bytes 8388608 | tf_op jit(solution)/shard_map/factor/pallas_call | solution.py:72
  297.8 1.9 copy-done.1
  299.7 0.8 copy-done.3
  300.5 2.2 fusion.8.mat_ref
  303.3 1.0 copy-done.4
  304.4 10.8 %solve.1 = f32[256,1024]{1,0:T(8,128)S(1)} custom-call(f32[256,1024]{1,0:T(8,128)S(1)} %fusion.8.mat_ref, f32[1024,1024]{1,0:T(8,128)S(1)} %copy-done.2, f32[1024,128]{1,0:T(8,128)S(1)} %copy-done.4), custom_call_target="tpu_custom_call" | custom-call | tf_op jit(solution)/shard_map/solve/pallas_call | solution.py:101
  315.1 1.1 compare_select_fusion.1
  (31 shorter events, 1.4 us)
Async XLA Ops:
  6.5 12.7 %copy-start = (bf16[512,3072]{1,0:T(8,128)(2,1)S(1)}, bf16[512,3072]{1,0:T(8,128)(2,1)}, u32[]{:S(2)}) copy-start(bf16[512,3072]{1,0:T(8,128)(2,1)} %param.5) | copy-start | bytes 9437188
  10.1 21.1 %all-to-all-start.1 = ((bf16[16,32,384]{2,1,0:T(8,128)(2,1)}), bf16[16,32,384]{2,1,0:T(8,128)(2,1)}, u32[]{:S(2)}, u32[]{:S(2)}) async-start(bf16[16,32,384]{2,1,0:T(8,128)(2,1)} %bitcast.6), calls=%async_computation.1 | async-start | bytes 786432 | tf_op jit(solution)/shard_map/all_to_all | solution.py:131
  18.5 157.4 %all-gather.6.cloned.1.call-start = ((), (), s32[]{:S(2)}) async-start(), calls=%async_computation.7 | async-start | bytes 7520256 | tf_op jit(solution)/shard_map/all_gather | solution.py:134
  32.8 180.0 %all-to-all-start = ((bf16[16,32,3072]{2,1,0:T(8,128)(2,1)}), bf16[16,32,3072]{2,1,0:T(8,128)(2,1)}, u32[]{:S(2)}, u32[]{:S(2)}) async-start(bf16[16,32,3072]{2,1,0:T(8,128)(2,1)} %bitcast.40), calls=%async_computation | async-start | bytes 6291456 | tf_op jit(solution)/shard_map/all_to_all | solution.py:162
  37.3 201.9 %all-gather.4.cloned.1.call-start = ((), (), s32[]{:S(2)}) async-start(), calls=%async_computation.5 | async-start | bytes 1572864 | tf_op jit(solution)/shard_map/all_gather | solution.py:139
  179.1 60.2 %all-reduce.3.cloned.1.call-start = ((), (), s32[]{:S(2)}) async-start(), calls=%async_computation.6 | async-start | bytes 8388608 | tf_op jit(solution)/shard_map/psum | solution.py:159
  212.6 87.9 %reduce-scatter.2.cloned.1.call-start = ((), (), s32[]{:S(2)}) async-start(), calls=%async_computation.4 | async-start | bytes 3145728 | tf_op jit(solution)/shard_map/reduce_scatter | solution.py:165
  233.3 5.0 %all-to-all-start.2 = ((bf16[2,256,256]{2,1,0:T(8,128)(2,1)}), bf16[2,256,256]{2,1,0:T(8,128)(2,1)S(1)}, u32[]{:S(2)}, u32[]{:S(2)}) async-start(bf16[2,256,256]{2,1,0:T(8,128)(2,1)} %bitcast.13), calls=%async_computation.3 | async-start | bytes 524288 | tf_op jit(solution)/shard_map/all_to_all | solution.py:166
  243.5 57.0 %copy-start.5 = (bf16[256,2,256]{0,2,1:T(8,128)(2,1)S(1)}, bf16[256,2,256]{0,2,1:T(8,128)(2,1)}, u32[]{:S(2)}) copy-start(bf16[256,2,256]{0,2,1:T(8,128)(2,1)} %copy.11) | copy-start | bytes 786436
  297.7 2.0 copy-start.1
  299.7 0.8 copy-start.3
  300.5 2.8 copy-start.2
  303.3 1.0 copy-start.4
Sparse Core Ops, SparseCore 0:
  33.0 142.9 all-gather.5
  179.2 7.0 all-gather.3
  212.7 26.3 all-reduce.2
  241.2 10.8 reduce-scatter.1
